TPU v7x, 32 devices: a whole 2x2x4 slice. The times are simulated.
32 devices in a mesh: shard: 4 (over y, x), ctx: 2 (over core), tp: 4 (over z).
Axes of the slice: x: 2, y: 2, z: 4, core: 2. Of those that a mesh axis runs over, the one named last changes fastest.
Arguments:
- activations: bfloat16 [4, 2048, 1024], P('shard', 'ctx'), may hold values from -6 to 6
- timestep: int32 [4], P('shard'), may hold values from 0 to 999
- positions: int32 [4, 2048], P('shard', 'ctx'), may hold values from 0 to 16383
- qkv_weight: bfloat16 [3, 1024, 1024], P(None, 'shard', 'tp'), may hold values from -0.1875 to 0.1875
- out_weight: bfloat16 [1024, 1024], P('tp', 'shard'), may hold values from -4 to 4
- up_weight: bfloat16 [1024, 4096], P('shard', 'tp'), may hold values from -0.1875 to 0.1875
- down_weight: bfloat16 [4096, 1024], P('tp', 'shard'), may hold values from -0.125 to 0.125
- time_weight: bfloat16 [256, 4, 1024], P(None, None, 'shard'), may hold values from -0.1875 to 0.1875
- norm_gains: bfloat16 [2, 1024], P(None, 'shard'), may hold values from 0.5 to 1.5
- cotangent: bfloat16 [4, 2048, 1024], P('shard', 'ctx'), may hold values from -6 to 6
Outputs:
- output: bfloat16 [4, 2048, 1024], P('shard', 'ctx')
- input_grad: bfloat16 [4, 2048, 1024], P('shard', 'ctx')
- grad_qkv: float32 [3, 1024, 1024], P(None, 'shard', 'tp')
- grad_out: float32 [1024, 1024], P('tp', 'shard')
- grad_up: float32 [1024, 4096], P('shard', 'tp')
- grad_down: float32 [4096, 1024], P('tp', 'shard')
- grad_time: float32 [256, 4, 1024], P(None, None, 'shard')
- grad_gains: float32 [2, 1024], P(None, 'shard')
All inputs are finite; a program needn't handle non-finite values.
Results may differ from a plain program's by a relative error of at most 0.015.
Values may be sent and summed in bfloat16 or wider, within the bound.
No kernel may reach another device: no remote copies, remote signals or barrier semaphores. Data moves between devices by JAX's collectives and lax.ppermute only.
A program may use at most 320 MiB of HBM per device.

v0:
```python
from functools import partial
import math
import jax
import jax.numpy as jnp
from jax import lax
from jax.sharding import PartitionSpec as P

HEAD_DIM = 64
TEMB = 256
highest = lax.Precision.HIGHEST
norm_epsilon = 1e-05


def embed_time(timestep):
    half_width = TEMB // 2
    frequency = jnp.exp(-math.log(10000.0) * jnp.arange(half_width, dtype=jnp.float32) / half_width)
    angles = timestep.astype(jnp.float32)[:, None] * frequency[None, :]
    return jnp.concatenate([jnp.sin(angles), jnp.cos(angles)], axis=-1)


def rotary_tables(positions):
    half_width = HEAD_DIM // 2
    frequency = jnp.exp(-math.log(10000.0) * jnp.arange(half_width, dtype=jnp.float32) / half_width)
    angles = positions.astype(jnp.float32)[..., None] * frequency
    return (jnp.cos(angles), jnp.sin(angles))


def rotate(heads_in, cosines, sines):
    half_width = HEAD_DIM // 2
    first = heads_in[..., :half_width]
    second = heads_in[..., half_width:]
    cos_wide = cosines[..., None, :]
    sin_wide = sines[..., None, :]
    return jnp.concatenate(
        [first * cos_wide - second * sin_wide, second * cos_wide + first * sin_wide], axis=-1
    )


def unrotate(heads_in, cosines, sines):
    half_width = HEAD_DIM // 2
    first = heads_in[..., :half_width]
    second = heads_in[..., half_width:]
    cos_wide = cosines[..., None, :]
    sin_wide = sines[..., None, :]
    return jnp.concatenate(
        [first * cos_wide + second * sin_wide, second * cos_wide - first * sin_wide], axis=-1
    )


def scaled_norm(values, gain_vec, scaling, offset):
    centered = values - jnp.mean(values, axis=-1, keepdims=True)
    variance = jnp.mean(centered * centered, axis=-1, keepdims=True)
    inverse_std = lax.rsqrt(variance + norm_epsilon)
    normed = centered * inverse_std
    return (
        normed * gain_vec * (1.0 + scaling[:, None, :]) + offset[:, None, :],
        normed,
        inverse_std,
    )


def norm_back(grad_in, normed, inverse_std, gain_vec, scaling):
    factor = gain_vec * (1.0 + scaling[:, None, :])
    grad_normed = grad_in * factor
    grad_values = inverse_std * (
        grad_normed
        - jnp.mean(grad_normed, axis=-1, keepdims=True)
        - normed * jnp.mean(grad_normed * normed, axis=-1, keepdims=True)
    )
    grad_gain = jnp.sum(grad_in * normed * (1.0 + scaling[:, None, :]), axis=(0, 1))
    grad_scaling = jnp.sum(grad_in * normed * gain_vec, axis=1)
    grad_offset = jnp.sum(grad_in, axis=1)
    return (grad_values, grad_gain, grad_scaling, grad_offset)


def group_heads(field, per_group):
    seq_count, rows_count, _ = field.shape
    split = field.reshape(seq_count, rows_count, -1, HEAD_DIM).transpose(0, 2, 1, 3)
    return split.reshape(-1, per_group, rows_count, HEAD_DIM)


def ungroup_heads(field, seq_count):
    rows_count = field.shape[2]
    joined = field.reshape(seq_count, -1, rows_count, HEAD_DIM).transpose(0, 2, 1, 3)
    return joined.reshape(seq_count, rows_count, -1)


def attend_block(triple, scaling):
    queries, keys, values = triple
    scores = jnp.einsum("gqd,gkd->gqk", queries, keys, preferred_element_type=jnp.float32) * scaling
    top_score = jnp.max(scores, axis=-1, keepdims=True)
    raised = jnp.exp(scores - top_score)
    total = jnp.sum(raised, axis=-1, keepdims=True)
    weights = (raised / total).astype(jnp.bfloat16)
    attended = jnp.einsum("gqk,gkd->gqd", weights, values, preferred_element_type=jnp.float32)
    return (attended, (top_score + jnp.log(total))[..., 0])


def attend_back(bundle, scaling):
    queries, keys, values, grad_out, log_total = bundle
    scores = jnp.einsum("gqd,gkd->gqk", queries, keys, preferred_element_type=jnp.float32) * scaling
    weights = jnp.exp(scores - log_total[..., None])
    grad_values = jnp.einsum(
        "gqk,gqd->gkd", weights.astype(jnp.bfloat16), grad_out, preferred_element_type=jnp.float32
    )
    grad_weights = jnp.einsum("gqd,gkd->gqk", grad_out, values, preferred_element_type=jnp.float32)
    row_term = jnp.sum(weights * grad_weights, axis=-1, keepdims=True)
    grad_scores = (weights * (grad_weights - row_term)).astype(jnp.bfloat16)
    grad_queries = (
        jnp.einsum("gqk,gkd->gqd", grad_scores, keys, preferred_element_type=jnp.float32) * scaling
    )
    grad_keys = (
        jnp.einsum("gqk,gqd->gkd", grad_scores, queries, preferred_element_type=jnp.float32)
        * scaling
    )
    return (grad_queries, grad_keys, grad_values)


def gelu_slope(hidden):
    return (
        0.5 * (1.0 + lax.erf(hidden * 0.7071067811865476))
        + hidden * jnp.exp(-0.5 * hidden * hidden) * 0.3989422804014327
    )


def body(
    activations,
    timestep,
    positions,
    qkv_weight,
    out_weight,
    up_weight,
    down_weight,
    time_weight,
    norm_gains,
    cotangent,
):
    seq_count, tokens, width = activations.shape
    local_width = qkv_weight.shape[2]
    heads_local = local_width // HEAD_DIM
    per_group = min(heads_local, max(1, 512 // tokens))
    while heads_local % per_group:
        per_group -= 1
    scaling = HEAD_DIM ** (-0.5)
    full_qkv, full_out, full_up, full_down, full_time, full_gains = (
        lax.all_gather(qkv_weight, "shard", axis=1, tiled=True),
        lax.all_gather(out_weight, "shard", axis=1, tiled=True),
        lax.all_gather(up_weight, "shard", axis=0, tiled=True),
        lax.all_gather(down_weight, "shard", axis=1, tiled=True),
        lax.all_gather(time_weight, "shard", axis=2, tiled=True),
        lax.all_gather(norm_gains, "shard", axis=1, tiled=True),
    )
    gains_f = full_gains.astype(jnp.float32)
    embedding = embed_time(timestep)
    modulation = jnp.einsum(
        "sk,kcd->scd", embedding, full_time.astype(jnp.float32), precision=highest
    )
    cosines, sines = rotary_tables(positions)
    inputs_f = activations.astype(jnp.float32)
    first_out, normed_one, inverse_one = scaled_norm(
        inputs_f, gains_f[0], modulation[:, 0], modulation[:, 1]
    )
    first_low = first_out.astype(jnp.bfloat16)
    projected = jnp.einsum("std,cde->cste", first_low, full_qkv, preferred_element_type=jnp.float32)
    head_shape = (seq_count, tokens, heads_local, HEAD_DIM)
    query_rot = (
        rotate(projected[0].reshape(head_shape), cosines, sines)
        .reshape(seq_count, tokens, local_width)
        .astype(jnp.bfloat16)
    )
    key_rot = (
        rotate(projected[1].reshape(head_shape), cosines, sines)
        .reshape(seq_count, tokens, local_width)
        .astype(jnp.bfloat16)
    )
    value_low = projected[2].astype(jnp.bfloat16)
    keys_all, values_all = (
        lax.all_gather(key_rot, "ctx", axis=1, tiled=True),
        lax.all_gather(value_low, "ctx", axis=1, tiled=True),
    )
    query_groups = group_heads(query_rot, per_group)
    attended, log_total = lax.map(
        partial(attend_block, scaling=scaling),
        (query_groups, group_heads(keys_all, per_group), group_heads(values_all, per_group)),
    )
    attended_low = ungroup_heads(attended, seq_count).astype(jnp.bfloat16)
    branch_part = jnp.einsum(
        "ste,ed->std", attended_low, full_out, preferred_element_type=jnp.float32
    )
    middle = inputs_f + lax.psum(branch_part, "tp")
    second_out, normed_two, inverse_two = scaled_norm(
        middle, gains_f[1], modulation[:, 2], modulation[:, 3]
    )
    second_low = second_out.astype(jnp.bfloat16)
    hidden = jnp.einsum("std,df->stf", second_low, full_up, preferred_element_type=jnp.float32)
    activated = jax.nn.gelu(hidden, approximate=False).astype(jnp.bfloat16)
    mlp_part = jnp.einsum("stf,fd->std", activated, full_down, preferred_element_type=jnp.float32)
    output = (middle + lax.psum(mlp_part, "tp")).astype(jnp.bfloat16)
    back_qkv, back_out, back_up, back_down = (
        lax.all_gather(qkv_weight, "shard", axis=1, tiled=True),
        lax.all_gather(out_weight, "shard", axis=1, tiled=True),
        lax.all_gather(up_weight, "shard", axis=0, tiled=True),
        lax.all_gather(down_weight, "shard", axis=1, tiled=True),
    )
    keys_back, values_back = (
        lax.all_gather(key_rot, "ctx", axis=1, tiled=True),
        lax.all_gather(value_low, "ctx", axis=1, tiled=True),
    )
    grad_down = jnp.einsum("stf,std->fd", activated, cotangent, preferred_element_type=jnp.float32)
    grad_act = jnp.einsum("std,fd->stf", cotangent, back_down, preferred_element_type=jnp.float32)
    grad_hidden = (grad_act * gelu_slope(hidden)).astype(jnp.bfloat16)
    grad_up = jnp.einsum("std,stf->df", second_low, grad_hidden, preferred_element_type=jnp.float32)
    grad_second = lax.psum(
        jnp.einsum("stf,df->std", grad_hidden, back_up, preferred_element_type=jnp.float32), "tp"
    )
    grad_mid_norm, gain_two, scaling_two, offset_two = norm_back(
        grad_second, normed_two, inverse_two, gains_f[1], modulation[:, 2]
    )
    grad_middle = cotangent.astype(jnp.float32) + grad_mid_norm
    grad_branch = grad_middle.astype(jnp.bfloat16)
    grad_out = jnp.einsum(
        "ste,std->ed", attended_low, grad_branch, preferred_element_type=jnp.float32
    )
    grad_attended = jnp.einsum(
        "std,ed->ste", grad_branch, back_out, preferred_element_type=jnp.float32
    ).astype(jnp.bfloat16)
    grad_query_g, grad_key_g, grad_value_g = lax.map(
        partial(attend_back, scaling=scaling),
        (
            query_groups,
            group_heads(keys_back, per_group),
            group_heads(values_back, per_group),
            group_heads(grad_attended, per_group),
            log_total,
        ),
    )
    grad_key_all = ungroup_heads(grad_key_g, seq_count)
    grad_value_all = ungroup_heads(grad_value_g, seq_count)
    grad_key, grad_value = (
        lax.psum_scatter(grad_key_all, "ctx", scatter_dimension=1, tiled=True),
        lax.psum_scatter(grad_value_all, "ctx", scatter_dimension=1, tiled=True),
    )
    grad_query = ungroup_heads(grad_query_g, seq_count)
    query_back = unrotate(grad_query.reshape(head_shape), cosines, sines).reshape(
        seq_count, tokens, local_width
    )
    key_back = unrotate(grad_key.reshape(head_shape), cosines, sines).reshape(
        seq_count, tokens, local_width
    )
    grad_projected = jnp.stack([query_back, key_back, grad_value], axis=0).astype(jnp.bfloat16)
    grad_qkv = jnp.einsum(
        "std,cste->cde", first_low, grad_projected, preferred_element_type=jnp.float32
    )
    grad_first = lax.psum(
        jnp.einsum("cste,cde->std", grad_projected, back_qkv, preferred_element_type=jnp.float32),
        "tp",
    )
    grad_in_norm, gain_one, scaling_one, offset_one = norm_back(
        grad_first, normed_one, inverse_one, gains_f[0], modulation[:, 0]
    )
    input_grad = (grad_middle + grad_in_norm).astype(jnp.bfloat16)
    grad_modulation = jnp.stack([scaling_one, offset_one, scaling_two, offset_two], axis=1)
    grad_time = jnp.einsum("sk,scd->kcd", embedding, grad_modulation, precision=highest)
    grad_gains = jnp.stack([gain_one, gain_two], axis=0)
    shares = (
        lax.psum_scatter(grad_qkv, "shard", scatter_dimension=1, tiled=True),
        lax.psum_scatter(grad_out, "shard", scatter_dimension=1, tiled=True),
        lax.psum_scatter(grad_up, "shard", scatter_dimension=0, tiled=True),
        lax.psum_scatter(grad_down, "shard", scatter_dimension=1, tiled=True),
        lax.psum_scatter(grad_time, "shard", scatter_dimension=2, tiled=True),
        lax.psum_scatter(grad_gains, "shard", scatter_dimension=1, tiled=True),
    )
    shares = lax.psum((shares[0], shares[1], shares[2], shares[3], shares[4], shares[5]), "ctx")
    return (output, input_grad, shares[0], shares[1], shares[2], shares[3], shares[4], shares[5])


def solution(mesh):
    placed = (
        P("shard", "ctx", None),
        P("shard"),
        P("shard", "ctx"),
        P(None, "shard", "tp"),
        P("tp", "shard"),
        P("shard", "tp"),
        P("tp", "shard"),
        P(None, None, "shard"),
        P(None, "shard"),
        P("shard", "ctx", None),
    )
    return jax.shard_map(
        body,
        mesh=mesh,
        in_specs=placed,
        out_specs=(
            P("shard", "ctx", None),
            P("shard", "ctx", None),
            P(None, "shard", "tp"),
            P("tp", "shard"),
            P("shard", "tp"),
            P("tp", "shard"),
            P(None, None, "shard"),
            P(None, "shard"),
        ),
        check_vma=False,
    )
```

profile of v0, /device:TPU:0, one launch (start us, length us, event | category | flops | bytes accessed | tf_op | source)
XLA Modules:
  0.0 1433.2 jit_solution(13286509616975945891)
XLA Ops:
  11.3 9.6 all_gather.30
  24.3 23.4 %all-gather.8.cloned.1.call-done = bf16[256,4,1024]{2,1,0:T(4,128)(2,1)} async-done(((bf16[256,4,256]{2,1,0:T(4,128)(2,1)}), bf16[256,4,1024]{2,1,0:T(4,128)(2,1)}) %all-gather.8.cloned.1.call-update) | async-done | bytes 2097168 | tf_op jit(solution)/shard_map/all_gather | solution.py:150
  51.8 29.2 %all-gather.10.cloned.1.call-done = bf16[3,1024,256]{1,2,0:T(8,128)(2,1)} async-done(((bf16[3,256,256]{1,2,0:T(8,128)(2,1)}), bf16[3,1024,256]{1,2,0:T(8,128)(2,1)}) %all-gather.10.cloned.1.call-update) | async-done | bytes 1572880 | tf_op jit(solution)/shard_map/all_gather | solution.py:146
  88.6 14.1 all_gather.35
  111.5 35.0 %while.28 = (s32[]{:T(128)}, bf16[4,1,1024,64]{2,3,1,0:T(8,128)(2,1)}, f32[4,1,1024]{2,1,0:T(1,128)S(1)}, bf16[4,1,1024,64]{3,2,1,0:T(8,128)(2,1)S(1)}, bf16[4,1...) while((s32[]{:T(128)}, bf16[4,1,1024,64]{2,3,1,0:T(8,128)(2,1)}, ...), condition=%wide.region_5.6_spmd.clone, body=%wide.region_2.5_spmd.sunk.clone | while | flops 555744256 | bytes 30976136 | solution.py:182
  151.9 153.9 %all-reduce.7.cloned.1.call-done = f32[1,1024,1024]{2,1,0:T(8,128)} async-done(((f32[1,1024,1024]{2,1,0:T(8,128)}), f32[1,1024,1024]{2,1,0:T(8,128)}) %all-reduce.7.cloned.1.call-update) | async-done | bytes 4194320 | tf_op jit(solution)/shard_map/psum | solution.py:190
  311.0 31.0 %all-gather.14.cloned.1.call-done = bf16[1024,1024]{1,0:T(8,128)(2,1)} async-done(((bf16[256,1024]{1,0:T(8,128)(2,1)}), bf16[1024,1024]{1,0:T(8,128)(2,1)}) %all-gather.14.cloned.1.call-update) | async-done | bytes 2097168 | tf_op jit(solution)/shard_map/all_gather | solution.py:148
  342.0 15.0 %fusion.66 = (bf16[1024,1024]{1,0:T(8,128)(2,1)}, f32[1024,1024]{1,0:T(8,128)}) fusion(bf16[1024,1024]{1,0:T(8,128)(2,1)} %all-gather.14.cloned.1.call-done, f32[1,1024,1024]{2,1,0:T(8,128)} %copy-done, f32[1024]{0:T(1024)S(1)} %bitcast.301, f32[1024]{0:T(1024)S(1)} %bitcast.283, f32[1024]{0:T(1024)S(1)} %bitcast.279, f32[1024]{0:T(1024)S(1)} %add_rsqrt_fusion, ...), kind=kOutput, calls=%fused_computation.77 | convolution fusion | flops 2221932544 | bytes 12603392 | tf_op jit(solution)/shard_map/std,df->stf/dot_general | solution.py:195
  356.9 22.2 %all-gather.16.cloned.1.call-done = bf16[1024,1024]{1,0:T(8,128)(2,1)} async-done(((bf16[1024,256]{1,0:T(8,128)(2,1)}), bf16[1024,1024]{1,0:T(8,128)(2,1)}) %all-gather.16.cloned.1.call-update) | async-done | bytes 2097168 | tf_op jit(solution)/shard_map/all_gather | solution.py:149
  391.3 154.9 %all-reduce.9.cloned.1.call-done = f32[1,1024,1024]{2,1,0:T(8,128)} async-done(((f32[1,1024,1024]{2,1,0:T(8,128)}), f32[1,1024,1024]{2,1,0:T(8,128)}) %all-reduce.9.cloned.1.call-update) | async-done | bytes 4194320 | tf_op jit(solution)/shard_map/psum | solution.py:213
  560.0 51.6 %while.29 = (s32[]{:T(128)}, f32[4,1,1024,64]{2,3,1,0:T(8,128)}, f32[4,1,2048,64]{2,3,1,0:T(8,128)}, f32[4,1,2048,64]{2,3,1,0:T(8,128)}, bf16[4,1,1024,64]{3,2,1...) while((s32[]{:T(128)}, f32[4,1,1024,64]{2,3,1,0:T(8,128)}, ...), condition=%wide.region_15.16_spmd.clone, body=%wide.region_13.15_spmd.sunk.clone | while | flops 1367538688 | bytes 68977792 | solution.py:227
  624.5 9.5 reduce-scatter.15.cloned.1.call-done
  641.2 292.3 %all-reduce.11.cloned.1.call-done = (f32[1,1024,1024]{2,1,0:T(8,128)}, f32[1,1024,1024]{2,1,0:T(8,128)}) async-done(((f32[1,1024,1024]{2,1,0:T(8,128)}, f32[1,1024,1024]{2,1,0:T(8,128)}), (f32[1,1024,1024]{2,1,0:T(8,128)}, f32[1,1024,1024]{2,1,0:T(8,128)})) %all-reduce.11.cloned.1.call-update) | async-done | bytes 8388624 | tf_op jit(solution)/shard_map/psum | solution.py:198
  940.3 64.8 %copy.59 = f32[256,4,1024]{1,0,2:T(8,128)} copy(f32[256,4,1024]{2,1,0:T(4,128)} %broadcast_multiply_fusion) | data formatting | bytes 8388608
  1005.1 110.5 %reshape.619 = f32[1024,1024]{1,0:T(8,128)} reshape(f32[1024,256,4]{2,1,0:T(8,128)} %bitcast.86) | data formatting | bytes 8388608
  1128.5 7.7 fusion.106
  1143.3 24.2 %reduce-scatter.25.cloned.1.call-done = f32[256,1024]{1,0:T(8,128)} async-done(((f32[1024,1024]{1,0:T(8,128)}), f32[256,1024]{1,0:T(8,128)}) %reduce-scatter.25.cloned.1.call-update) | async-done | bytes 1048592
  1167.5 36.8 %reshape.620 = f32[256,256,4]{2,1,0:T(8,128)} reshape(f32[256,1024]{1,0:T(8,128)} %reduce-scatter.25.cloned.1.call-done) | data formatting | bytes 2097152
  1204.3 21.0 %copy.60 = f32[256,4,256]{2,1,0:T(4,128)} copy(f32[256,4,256]{1,0,2:T(8,128)} %bitcast.252) | data formatting | bytes 2097152
  1225.3 29.1 %reduce-scatter.23.cloned.1.call-done = f32[1024,256]{1,0:T(8,128)} async-done(((f32[1024,1024]{1,0:T(8,128)}), f32[1024,256]{1,0:T(8,128)}) %reduce-scatter.23.cloned.1.call-update) | async-done | bytes 1048592 | tf_op jit(solution)/shard_map/reduce_scatter | solution.py:269
  1254.5 55.8 %reduce-scatter.21.cloned.1.call-done = f32[256,1024]{1,0:T(8,128)} async-done(((f32[1024,1024]{1,0:T(8,128)}), f32[256,1024]{1,0:T(8,128)}) %reduce-scatter.21.cloned.1.call-update) | async-done | bytes 1048592 | tf_op jit(solution)/shard_map/reduce_scatter | solution.py:268
  1310.3 46.8 %reduce-scatter.17.cloned.1.call-done = f32[3,256,256]{1,2,0:T(8,128)} async-done(((f32[3,1024,256]{1,2,0:T(8,128)}), f32[3,256,256]{1,2,0:T(8,128)}) %reduce-scatter.17.cloned.1.call-update) | async-done | bytes 786448 | tf_op jit(solution)/shard_map/reduce_scatter | solution.py:266
  1366.4 18.8 %reduce-scatter.27.cloned.1.call-done = f32[256,2]{1,0:T(8,128)} async-done(((f32[1024,2]{1,0:T(8,128)}), f32[256,2]{1,0:T(8,128)}) %reduce-scatter.27.cloned.1.call-update) | async-done | bytes 2064
  1389.2 28.7 %all-reduce.13.cloned.1.call-done = (f32[3,256,256]{1,2,0:T(8,128)}, f32[256,256]{1,0:T(8,128)}, f32[256,1024]{1,0:T(8,128)}, f32[1024,256]{1,0:T(8,128)}, f32[256,4,256]{2,1,0:T(4,128)}) async-done(((f32[3,256,256]{1,2,0:T(8,128)}, f32[256,256]{1,0:T(8,128)}, f32[256,1024]{1,0:T(8,128)}, f32[1024,256]{1,0:T(8,128)}, f32[256,4,256]{2,1,0:T(4,128)}), (f32[3,256,256]{1,2,0:T(8,128)}, f32[256,256]{1,0:T(8,128)}, ...) | async-done | bytes 4194320 | tf_op jit(solution)/shard_map/psum | solution.py:273
  (286 shorter events, 217.9 us)
Async XLA Ops:
  7.2 40.6 %all-gather.8.cloned.1.call-start = ((), (), s32[]{:S(2)}) async-start(), calls=%async_computation.8 | async-start | bytes 2621440 | tf_op jit(solution)/shard_map/all_gather | solution.py:150
  7.9 73.1 %all-gather.10.cloned.1.call-start = ((), (), s32[]{:S(2)}) async-start(), calls=%async_computation.9 | async-start | bytes 1966080 | tf_op jit(solution)/shard_map/all_gather | solution.py:146
  9.9 96.0 %all-gather.12.cloned.1.call-start = ((), (), s32[]{:S(2)}) async-start(), calls=%async_computation.10 | async-start | bytes 1572864 | tf_op jit(solution)/shard_map/all_gather | solution.py:178
  23.8 522.3 %copy-start.36 = (f32[1,1024]{1,0:T(1,128)}, f32[1,1024]{1,0:T(1,128)S(1)}, u32[]{:S(2)}) copy-start(f32[1,1024]{1,0:T(1,128)S(1)} %get-tuple-element.239) | copy-start | bytes 12292
  51.8 494.3 %copy-start.39 = (f32[1,1,1024]{2,1,0:T(1,128)}, f32[1,1,1024]{2,1,0:T(1,128)S(1)}, u32[]{:S(2)}) copy-start(f32[1,1,1024]{2,1,0:T(1,128)S(1)} %get-tuple-element.233) | copy-start | bytes 12292
  86.3 22.4 %all-gather.18.cloned.1.call-start = ((), (), s32[]{:S(2)}) async-start(), calls=%async_computation.21 | async-start | bytes 1572864 | tf_op jit(solution)/shard_map/all_gather | solution.py:179
  88.5 217.2 %all-reduce.7.cloned.1.call-start = ((), (), s32[]{:S(2)}) async-start(), calls=%async_computation.11 | async-start | bytes 8388608 | tf_op jit(solution)/shard_map/psum | solution.py:190
  150.5 191.5 %all-gather.14.cloned.1.call-start = ((), (), s32[]{:S(2)}) async-start(), calls=%async_computation.12 | async-start | bytes 2621440 | tf_op jit(solution)/shard_map/all_gather | solution.py:148
  151.1 228.0 %all-gather.16.cloned.1.call-start = ((), (), s32[]{:S(2)}) async-start(), calls=%async_computation.13 | async-start | bytes 2621440 | tf_op jit(solution)/shard_map/all_gather | solution.py:149
  151.8 394.3 %all-reduce.9.cloned.1.call-start = ((), (), s32[]{:S(2)}) async-start(), calls=%async_computation.14 | async-start | bytes 8388608 | tf_op jit(solution)/shard_map/psum | solution.py:213
  391.0 231.4 %reduce-scatter.13.cloned.1.call-start = ((), (), s32[]{:S(2)}) async-start(), calls=%async_computation.15 | async-start | bytes 3145728 | tf_op jit(solution)/shard_map/reduce_scatter | solution.py:240
  611.6 22.4 %reduce-scatter.15.cloned.1.call-start = ((), (), s32[]{:S(2)}) async-start(), calls=%async_computation.16 | async-start | bytes 3145728 | tf_op jit(solution)/shard_map/reduce_scatter | solution.py:241
  614.6 318.9 %all-reduce.11.cloned.1.call-start = ((), (), s32[]{:S(2)}) async-start(), calls=%async_computation.24 | async-start | bytes 16777216 | tf_op jit(solution)/shard_map/psum | solution.py:198
  640.5 292.9 %copy-start.5 = (bf16[1,1024,1024]{2,1,0:T(8,128)(2,1)S(1)}, bf16[1,1024,1024]{2,1,0:T(8,128)(2,1)}, u32[]{:S(2)}) copy-start(bf16[1,1024,1024]{2,1,0:T(8,128)(2,1)} %param.14) | copy-start | bytes 6291460
  640.5 292.9 %copy-start.30 = (f32[1024]{0:T(1024)S(1)}, f32[1024]{0:T(1024)}, u32[]{:S(2)}) copy-start(f32[1024]{0:T(1024)} %copy-done.29) | copy-start | bytes 12292
  640.5 292.9 %copy-start.34 = (f32[1024]{0:T(1024)S(1)}, f32[1024]{0:T(1024)}, u32[]{:S(2)}) copy-start(f32[1024]{0:T(1024)} %copy-done.33) | copy-start | bytes 12292
  640.5 292.9 %copy-start.35 = (f32[1,1,1024]{2,1,0:T(1,128)S(1)}, f32[1,1,1024]{2,1,0:T(1,128)}, u32[]{:S(2)}) copy-start(f32[1,1,1024]{2,1,0:T(1,128)} %get-tuple-element.231) | copy-start | bytes 12292
  640.6 526.9 %reduce-scatter.25.cloned.1.call-start = ((), (), s32[]{:S(2)}) async-start(), calls=%async_computation.22 | async-start | bytes 5242880
  1115.6 109.7 %reduce-scatter.19.cloned.1.call-start = ((), (), s32[]{:S(2)}) async-start(), calls=%async_computation.18 | async-start | bytes 1310720 | tf_op jit(solution)/shard_map/reduce_scatter | solution.py:267
  1120.5 134.0 %reduce-scatter.23.cloned.1.call-start = ((), (), s32[]{:S(2)}) async-start(), calls=%async_computation.20 | async-start | bytes 5242880 | tf_op jit(solution)/shard_map/reduce_scatter | solution.py:269
  1127.9 182.4 %reduce-scatter.21.cloned.1.call-start = ((), (), s32[]{:S(2)}) async-start(), calls=%async_computation.19 | async-start | bytes 5242880 | tf_op jit(solution)/shard_map/reduce_scatter | solution.py:268
  1136.3 220.8 %reduce-scatter.17.cloned.1.call-start = ((), (), s32[]{:S(2)}) async-start(), calls=%async_computation.17 | async-start | bytes 3932160 | tf_op jit(solution)/shard_map/reduce_scatter | solution.py:266
  1142.1 243.0 %reduce-scatter.27.cloned.1.call-start = ((), (), s32[]{:S(2)}) async-start(), calls=%async_computation.23 | async-start | bytes 655360
  1143.3 274.5 %all-reduce.13.cloned.1.call-start = ((), (), s32[]{:S(2)}) async-start(), calls=%async_computation.25 | async-start | bytes 8388608 | tf_op jit(solution)/shard_map/psum | solution.py:273
  (58 other events, 1990.5 us)
Sparse Core Ops, SparseCore 0:
  9.8 37.8 all-gather.7
  50.1 30.8 all-gather.9
  86.5 9.0 all-gather.11
  97.5 10.1 all-gather.17
  150.6 155.0 all-reduce.6
  307.6 34.3 all-gather.13
  343.9 35.1 all-gather.15
  391.1 154.9 all-reduce.8
  611.7 8.5 reduce-scatter.12
  623.1 10.8 reduce-scatter.14
  640.7 292.6 all-reduce.10
  1115.7 51.7 reduce-scatter.24
  1171.2 27.6 reduce-scatter.18
  1201.8 52.6 reduce-scatter.22
  1257.6 52.6 reduce-scatter.20
  1313.1 43.9 reduce-scatter.16
  1360.4 24.7 reduce-scatter.26
  1388.8 28.9 all-reduce.12
where the time goes:
time: 1440 us; the launch traced here: 1430 us
  waiting for transfers between devices  922 us (64%)
  local copies, waits for them, and re-layouts  273 us (19%)
  matrix products  141 us (10%)
  other arithmetic  53.4 us (4%)
  blocking collectives  26.7 us (2%)
  between operations  15.8 us (1%)
    psum x1, waiting for transfers between devices, body(): output = (middle + lax.psum(mlp_part, 'tp')).astype(jnp.bfloat16)  292 us
    unnamed x116, local copies, waits for them, and re-layouts  255 us
    psum x1, waiting for transfers between devices, body(): lax.psum(jnp.einsum('stf,df->std', grad_hidden, back_up, preferred_elemen...  155 us
    psum x1, waiting for transfers between devices, body(): middle = inputs_f + lax.psum(branch_part, 'tp')  154 us
    reduce_scatter x1, waiting for transfers between devices, body(): lax.psum_scatter(grad_up, 'shard', scatter_dimension=0, tiled=True)  55.8 us
    reduce_scatter x1, waiting for transfers between devices, body(): lax.psum_scatter(grad_qkv, 'shard', scatter_dimension=1, tiled=True)  46.8 us
    unnamed x20, waiting for transfers between devices  44.9 us
    all_gather x1, waiting for transfers between devices, body(): lax.all_gather(up_weight, 'shard', axis=0, tiled=True)  31 us
  transfers between devices with their start and end apart: 18, of which 14 were waited for; matrix products, arithmetic and copies ran while one was open for 10% of the time, Pallas kernels for 0%

commit v1 on v0

--- a/solution.py
+++ b/solution.py
@@ -9,6 +9,11 @@
 TEMB = 256
 highest = lax.Precision.HIGHEST
 norm_epsilon = 1e-05
+
+
+def summed_here(value, mesh_axis):
+    parts = lax.all_gather(value, mesh_axis)
+    return jnp.sum(parts, axis=0)
 
 
 def embed_time(timestep):
@@ -187,7 +192,7 @@
     branch_part = jnp.einsum(
         "ste,ed->std", attended_low, full_out, preferred_element_type=jnp.float32
     )
-    middle = inputs_f + lax.psum(branch_part, "tp")
+    middle = inputs_f + summed_here(branch_part, "tp")
     second_out, normed_two, inverse_two = scaled_norm(
         middle, gains_f[1], modulation[:, 2], modulation[:, 3]
     )

time: 1440 us -> 1580 us (1.097)
  waiting for transfers between devices: 922 us -> 1040 us
    all_gather x0 -> x1, waiting for transfers between devices: none -> 286 us  [summed_here(): parts = lax.all_gather(value, mesh_axis)]
    psum x1 -> x0, waiting for transfers between devices: 154 us -> none  [body(): middle = inputs_f + lax.psum(branch_part, 'tp')]
where the time goes in v1:
time: 1580 us; the launch traced here: 1560 us
  waiting for transfers between devices  1040 us (66%)
  local copies, waits for them, and re-layouts  273 us (17%)
  matrix products  141 us (9%)
  other arithmetic  63.7 us (4%)
  blocking collectives  26.7 us (2%)
  between operations  15.8 us (1%)
    psum x1, waiting for transfers between devices, body(): output = (middle + lax.psum(mlp_part, 'tp')).astype(jnp.bfloat16)  292 us
    all_gather x1, waiting for transfers between devices, summed_here(): parts = lax.all_gather(value, mesh_axis)  286 us
    unnamed x116, local copies, waits for them, and re-layouts  255 us
    psum x1, waiting for transfers between devices, body(): lax.psum(jnp.einsum('stf,df->std', grad_hidden, back_up, preferred_elemen...  155 us
    reduce_scatter x1, waiting for transfers between devices, body(): lax.psum_scatter(grad_up, 'shard', scatter_dimension=0, tiled=True)  55.6 us
    reduce_scatter x1, waiting for transfers between devices, body(): lax.psum_scatter(grad_qkv, 'shard', scatter_dimension=1, tiled=True)  47.1 us
    unnamed x20, waiting for transfers between devices  45.2 us
  transfers between devices with their start and end apart: 18, of which 14 were waited for; matrix products, arithmetic and copies ran while one was open for 10% of the time, Pallas kernels for 0%

profile of v1, /device:TPU:0, one launch (start us, length us, event | category | flops | bytes accessed | tf_op | source)
XLA Modules:
  0.0 1563.7 jit_solution(8406092710572245599)
XLA Ops:
  11.3 9.6 all_gather.36
  24.3 23.4 %all-gather.10.cloned.1.call-done = bf16[256,4,1024]{2,1,0:T(4,128)(2,1)} async-done(((bf16[256,4,256]{2,1,0:T(4,128)(2,1)}), bf16[256,4,1024]{2,1,0:T(4,128)(2,1)}) %all-gather.10.cloned.1.call-update) | async-done | bytes 2097168 | tf_op jit(solution)/shard_map/all_gather | solution.py:155
  51.8 29.2 %all-gather.12.cloned.1.call-done = bf16[3,1024,256]{1,2,0:T(8,128)(2,1)} async-done(((bf16[3,256,256]{1,2,0:T(8,128)(2,1)}), bf16[3,1024,256]{1,2,0:T(8,128)(2,1)}) %all-gather.12.cloned.1.call-update) | async-done | bytes 1572880 | tf_op jit(solution)/shard_map/all_gather | solution.py:151
  88.6 14.1 all_gather.41
  111.5 35.0 %while.28 = (s32[]{:T(128)}, bf16[4,1,1024,64]{2,3,1,0:T(8,128)(2,1)}, f32[4,1,1024]{2,1,0:T(1,128)S(1)}, bf16[4,1,1024,64]{3,2,1,0:T(8,128)(2,1)S(1)}, bf16[4,1...) while((s32[]{:T(128)}, bf16[4,1,1024,64]{2,3,1,0:T(8,128)(2,1)}, ...), condition=%wide.region_5.6_spmd.clone, body=%wide.region_2.5_spmd.sunk.clone | while | flops 555744256 | bytes 30976136 | solution.py:187
  151.8 285.7 %all-gather.22.cloned.1.call-done = f32[4096,1024]{1,0:T(8,128)} async-done(((f32[1024,1024]{1,0:T(8,128)}), f32[4096,1024]{1,0:T(8,128)}) %all-gather.22.cloned.1.call-update) | async-done | bytes 16777232 | tf_op jit(solution)/shard_map/all_gather | solution.py:15
  437.5 10.3 reduce.19
  453.1 19.7 %all-gather.16.cloned.1.call-done = bf16[1024,1024]{1,0:T(8,128)(2,1)} async-done(((bf16[256,1024]{1,0:T(8,128)(2,1)}), bf16[1024,1024]{1,0:T(8,128)(2,1)}) %all-gather.16.cloned.1.call-update) | async-done | bytes 2097168 | tf_op jit(solution)/shard_map/all_gather | solution.py:153
  472.7 15.0 fusion.66
  487.7 22.1 %all-gather.18.cloned.1.call-done = bf16[1024,1024]{1,0:T(8,128)(2,1)} async-done(((bf16[1024,256]{1,0:T(8,128)(2,1)}), bf16[1024,1024]{1,0:T(8,128)(2,1)}) %all-gather.18.cloned.1.call-update) | async-done | bytes 2097168 | tf_op jit(solution)/shard_map/all_gather | solution.py:154
  521.9 154.9 %all-reduce.6.cloned.1.call-done = f32[1,1024,1024]{2,1,0:T(8,128)} async-done(((f32[1,1024,1024]{2,1,0:T(8,128)}), f32[1,1024,1024]{2,1,0:T(8,128)}) %all-reduce.6.cloned.1.call-update) | async-done | bytes 4194320 | tf_op jit(solution)/shard_map/psum | solution.py:218
  690.6 51.6 %while.29 = (s32[]{:T(128)}, f32[4,1,1024,64]{2,3,1,0:T(8,128)}, f32[4,1,2048,64]{2,3,1,0:T(8,128)}, f32[4,1,2048,64]{2,3,1,0:T(8,128)}, bf16[4,1,1024,64]{3,2,1...) while((s32[]{:T(128)}, f32[4,1,1024,64]{2,3,1,0:T(8,128)}, ...), condition=%wide.region_15.16_spmd.clone, body=%wide.region_13.15_spmd.sunk.clone | while | flops 1367538688 | bytes 68977792 | solution.py:232
  755.1 9.4 reduce-scatter.15.cloned.1.call-done
  771.7 292.3 %all-reduce.8.cloned.1.call-done = (f32[1,1024,1024]{2,1,0:T(8,128)}, f32[1,1024,1024]{2,1,0:T(8,128)}) async-done(((f32[1,1024,1024]{2,1,0:T(8,128)}, f32[1,1024,1024]{2,1,0:T(8,128)}), (f32[1,1024,1024]{2,1,0:T(8,128)}, f32[1,1024,1024]{2,1,0:T(8,128)})) %all-reduce.8.cloned.1.call-update) | async-done | bytes 8388624 | tf_op jit(solution)/shard_map/psum | solution.py:203
  1070.8 64.8 %copy.59 = f32[256,4,1024]{1,0,2:T(8,128)} copy(f32[256,4,1024]{2,1,0:T(4,128)} %broadcast_multiply_fusion) | data formatting | bytes 8388608
  1135.6 110.5 %reshape.623 = f32[1024,1024]{1,0:T(8,128)} reshape(f32[1024,256,4]{2,1,0:T(8,128)} %bitcast.87) | data formatting | bytes 8388608
  1273.9 24.2 %reduce-scatter.25.cloned.1.call-done = f32[256,1024]{1,0:T(8,128)} async-done(((f32[1024,1024]{1,0:T(8,128)}), f32[256,1024]{1,0:T(8,128)}) %reduce-scatter.25.cloned.1.call-update) | async-done | bytes 1048592
  1298.0 36.8 %reshape.624 = f32[256,256,4]{2,1,0:T(8,128)} reshape(f32[256,1024]{1,0:T(8,128)} %reduce-scatter.25.cloned.1.call-done) | data formatting | bytes 2097152
  1334.8 21.0 %copy.60 = f32[256,4,256]{2,1,0:T(4,128)} copy(f32[256,4,256]{1,0,2:T(8,128)} %bitcast.254) | data formatting | bytes 2097152
  1355.8 29.2 %reduce-scatter.23.cloned.1.call-done = f32[1024,256]{1,0:T(8,128)} async-done(((f32[1024,1024]{1,0:T(8,128)}), f32[1024,256]{1,0:T(8,128)}) %reduce-scatter.23.cloned.1.call-update) | async-done | bytes 1048592 | tf_op jit(solution)/shard_map/reduce_scatter | solution.py:274
  1385.0 55.6 %reduce-scatter.21.cloned.1.call-done = f32[256,1024]{1,0:T(8,128)} async-done(((f32[1024,1024]{1,0:T(8,128)}), f32[256,1024]{1,0:T(8,128)}) %reduce-scatter.21.cloned.1.call-update) | async-done | bytes 1048592 | tf_op jit(solution)/shard_map/reduce_scatter | solution.py:273
  1440.6 47.1 %reduce-scatter.17.cloned.1.call-done = f32[3,256,256]{1,2,0:T(8,128)} async-done(((f32[3,1024,256]{1,2,0:T(8,128)}), f32[3,256,256]{1,2,0:T(8,128)}) %reduce-scatter.17.cloned.1.call-update) | async-done | bytes 786448 | tf_op jit(solution)/shard_map/reduce_scatter | solution.py:271
  1496.9 19.0 %reduce-scatter.27.cloned.1.call-done = f32[256,2]{1,0:T(8,128)} async-done(((f32[1024,2]{1,0:T(8,128)}), f32[256,2]{1,0:T(8,128)}) %reduce-scatter.27.cloned.1.call-update) | async-done | bytes 2064
  1520.0 28.3 %all-reduce.10.cloned.1.call-done = (f32[3,256,256]{1,2,0:T(8,128)}, f32[256,256]{1,0:T(8,128)}, f32[256,1024]{1,0:T(8,128)}, f32[1024,256]{1,0:T(8,128)}, f32[256,4,256]{2,1,0:T(4,128)}) async-done(((f32[3,256,256]{1,2,0:T(8,128)}, f32[256,256]{1,0:T(8,128)}, f32[256,1024]{1,0:T(8,128)}, f32[1024,256]{1,0:T(8,128)}, f32[256,4,256]{2,1,0:T(4,128)}), (f32[3,256,256]{1,2,0:T(8,128)}, f32[256,256]{1,0:T(8,128)}, ...) | async-done | bytes 4194320 | tf_op jit(solution)/shard_map/psum | solution.py:278
  (287 shorter events, 225.6 us)
Async XLA Ops:
  7.2 40.6 %all-gather.10.cloned.1.call-start = ((), (), s32[]{:S(2)}) async-start(), calls=%async_computation.8 | async-start | bytes 2621440 | tf_op jit(solution)/shard_map/all_gather | solution.py:155
  7.9 73.1 %all-gather.12.cloned.1.call-start = ((), (), s32[]{:S(2)}) async-start(), calls=%async_computation.9 | async-start | bytes 1966080 | tf_op jit(solution)/shard_map/all_gather | solution.py:151
  9.9 96.0 %all-gather.14.cloned.1.call-start = ((), (), s32[]{:S(2)}) async-start(), calls=%async_computation.10 | async-start | bytes 1572864 | tf_op jit(solution)/shard_map/all_gather | solution.py:183
  23.8 653.0 %copy-start.36 = (f32[1,1024]{1,0:T(1,128)}, f32[1,1024]{1,0:T(1,128)S(1)}, u32[]{:S(2)}) copy-start(f32[1,1024]{1,0:T(1,128)S(1)} %get-tuple-element.239) | copy-start | bytes 12292
  51.2 421.5 %copy-start.47 = (f32[1,1,1024]{2,0,1:T(1,128)}, f32[1,1,1024]{2,0,1:T(1,128)S(1)}, u32[]{:S(2)}) copy-start(f32[1,1,1024]{2,0,1:T(1,128)S(1)} %get-tuple-element.235) | copy-start | bytes 12292
  51.8 624.9 %copy-start.39 = (f32[1,1,1024]{2,1,0:T(1,128)}, f32[1,1,1024]{2,1,0:T(1,128)S(1)}, u32[]{:S(2)}) copy-start(f32[1,1,1024]{2,1,0:T(1,128)S(1)} %get-tuple-element.233) | copy-start | bytes 12292
  86.3 22.4 %all-gather.20.cloned.1.call-start = ((), (), s32[]{:S(2)}) async-start(), calls=%async_computation.20 | async-start | bytes 1572864 | tf_op jit(solution)/shard_map/all_gather | solution.py:184
  88.5 349.0 %all-gather.22.cloned.1.call-start = ((), (), s32[]{:S(2)}) async-start(), calls=%async_computation.21 | async-start | bytes 20971520 | tf_op jit(solution)/shard_map/all_gather | solution.py:15
  150.4 322.3 %all-gather.16.cloned.1.call-start = ((), (), s32[]{:S(2)}) async-start(), calls=%async_computation.11 | async-start | bytes 2621440 | tf_op jit(solution)/shard_map/all_gather | solution.py:153
  151.0 358.7 %all-gather.18.cloned.1.call-start = ((), (), s32[]{:S(2)}) async-start(), calls=%async_computation.12 | async-start | bytes 2621440 | tf_op jit(solution)/shard_map/all_gather | solution.py:154
  151.8 525.0 %all-reduce.6.cloned.1.call-start = ((), (), s32[]{:S(2)}) async-start(), calls=%async_computation.13 | async-start | bytes 8388608 | tf_op jit(solution)/shard_map/psum | solution.py:218
  521.6 231.4 %reduce-scatter.13.cloned.1.call-start = ((), (), s32[]{:S(2)}) async-start(), calls=%async_computation.14 | async-start | bytes 3145728 | tf_op jit(solution)/shard_map/reduce_scatter | solution.py:245
  742.3 22.2 %reduce-scatter.15.cloned.1.call-start = ((), (), s32[]{:S(2)}) async-start(), calls=%async_computation.15 | async-start | bytes 3145728 | tf_op jit(solution)/shard_map/reduce_scatter | solution.py:246
  745.2 318.8 %all-reduce.8.cloned.1.call-start = ((), (), s32[]{:S(2)}) async-start(), calls=%async_computation.24 | async-start | bytes 16777216 | tf_op jit(solution)/shard_map/psum | solution.py:203
  771.0 293.0 %copy-start.5 = (bf16[1,1024,1024]{2,1,0:T(8,128)(2,1)S(1)}, bf16[1,1024,1024]{2,1,0:T(8,128)(2,1)}, u32[]{:S(2)}) copy-start(bf16[1,1024,1024]{2,1,0:T(8,128)(2,1)} %param.14) | copy-start | bytes 6291460
  771.1 293.0 %copy-start.30 = (f32[1024]{0:T(1024)S(1)}, f32[1024]{0:T(1024)}, u32[]{:S(2)}) copy-start(f32[1024]{0:T(1024)} %copy-done.29) | copy-start | bytes 12292
  771.1 292.9 %copy-start.34 = (f32[1024]{0:T(1024)S(1)}, f32[1024]{0:T(1024)}, u32[]{:S(2)}) copy-start(f32[1024]{0:T(1024)} %copy-done.33) | copy-start | bytes 12292
  771.1 526.9 %reduce-scatter.25.cloned.1.call-start = ((), (), s32[]{:S(2)}) async-start(), calls=%async_computation.22 | async-start | bytes 5242880
  1246.2 109.7 %reduce-scatter.19.cloned.1.call-start = ((), (), s32[]{:S(2)}) async-start(), calls=%async_computation.17 | async-start | bytes 1310720 | tf_op jit(solution)/shard_map/reduce_scatter | solution.py:272
  1251.1 134.0 %reduce-scatter.23.cloned.1.call-start = ((), (), s32[]{:S(2)}) async-start(), calls=%async_computation.19 | async-start | bytes 5242880 | tf_op jit(solution)/shard_map/reduce_scatter | solution.py:274
  1258.4 182.2 %reduce-scatter.21.cloned.1.call-start = ((), (), s32[]{:S(2)}) async-start(), calls=%async_computation.18 | async-start | bytes 5242880 | tf_op jit(solution)/shard_map/reduce_scatter | solution.py:273
  1266.8 220.8 %reduce-scatter.17.cloned.1.call-start = ((), (), s32[]{:S(2)}) async-start(), calls=%async_computation.16 | async-start | bytes 3932160 | tf_op jit(solution)/shard_map/reduce_scatter | solution.py:271
  1272.7 243.3 %reduce-scatter.27.cloned.1.call-start = ((), (), s32[]{:S(2)}) async-start(), calls=%async_computation.23 | async-start | bytes 655360
  1273.8 274.5 %all-reduce.10.cloned.1.call-start = ((), (), s32[]{:S(2)}) async-start(), calls=%async_computation.25 | async-start | bytes 8388608 | tf_op jit(solution)/shard_map/psum | solution.py:278
  (58 other events, 1969.5 us)
Sparse Core Ops, SparseCore 0:
  9.8 37.8 all-gather.9
  50.1 30.8 all-gather.11
  86.5 9.0 all-gather.13
  97.5 10.1 all-gather.19
  150.6 286.9 all-gather.21
  439.2 33.4 all-gather.15
  474.6 35.1 all-gather.17
  521.7 154.9 all-reduce.5
  742.4 8.5 reduce-scatter.12
  753.7 10.7 reduce-scatter.14
  771.3 292.7 all-reduce.7
  1246.3 51.7 reduce-scatter.24
  1301.5 27.7 reduce-scatter.18
  1332.4 52.6 reduce-scatter.22
  1387.9 52.6 reduce-scatter.20
  1443.7 43.9 reduce-scatter.16
  1491.1 24.7 reduce-scatter.26
  1519.4 28.8 all-reduce.9
